TPU v7x, 32 devices: a whole 2x2x4 slice. The times are simulated.
32 devices in a mesh: rock: 4 (over y, x), frac: 8 (over z, core).
Axes of the slice: x: 2, y: 2, z: 4, core: 2. Of those that a mesh axis runs over, the one named last changes fastest.
Arguments:
- jumps: float32 [3, 32768, 128], P(None, ('rock', 'frac')), may hold values from -6 to 6
- base_aperture: float32 [32768, 128], P(('rock', 'frac')), may hold values from 1 to 3
- pressure: float32 [16, 32768, 128], P(None, ('rock', 'frac')), may hold values from -6 to 6
- block_fracture: int32 [32768], P(('rock', 'frac')), may hold values from 0 to 4095, never falling along the last dimension, each value on 1 to 32 neighbouring positions
- send_face: int32 [65536], P(('rock', 'frac')), may hold values from 0 to 1024, as said below
- elem_source: int32 [32768], P(('rock', 'frac')), may hold values from 0 to 2047, as said below
- pair_local: int32 [2048], P(('rock', 'frac')), may hold values from 0 to 1024, as said below
- send_block: int32 [2048], P(('rock', 'frac')), may hold values from 0 to 1024, as said below
- tiles: bfloat16 [2048, 128, 128], P(('rock', 'frac')), may hold values from 0 to 0.015625
Outputs:
- image: float32 [16, 32768, 128], P(None, ('rock', 'frac'))
- aperture: float32 [32768, 128], P(('rock', 'frac'))
Inputs may be any that keep to these rules, and one draw needn't show every extreme that they name: `send_face`: entry r * 512 + m of a device's block names the local face block that it sends as the m-th to the device of rock index r in its frac column, or 1024 for an empty slot; each face block is sent once; every device fills all 512 slots to one destination and receives 512 from one source. `elem_source`: the entry s * 512 + m of an element block names slot m of what the device of rock index s in the same frac column sends to its device; every filled slot is named once and no empty one. `pair_local`: entry q * 8 + c of a device's block is the local element block of its c-th intersection with the device of frac index q in its rock row, or 1024 for an empty slot; each device fills all 8 slots to at least one peer. `send_block`: entry q * 8 + c of a device's block is its local element block in the c-th intersection stored by the device of frac index q in the same rock row; it is 1024 exactly when that slot there is empty.
All inputs are finite; a program needn't handle non-finite values.
Results may differ from a plain program's by a relative error of at most 0.0003.
Values sent between devices are 32-bit elements; how exact they have to be, the bound alone decides.
A program may use at most 128 MiB of HBM per device.

v0:
```python
import jax
import jax.numpy as jnp
from jax import lax
from jax.sharding import PartitionSpec as P


def padded(cells, sides, width):
    for axis, dim in sides:
        count = lax.axis_size(axis)
        ends = count - 1
        head = lax.slice_in_dim(cells, 0, width, axis=dim)
        tail = lax.slice_in_dim(cells, cells.shape[dim] - width, cells.shape[dim], axis=dim)
        cells = jnp.concatenate(
            [
                lax.ppermute(tail, axis, [(i, (i + 1) % count) for i in range(ends)]),
                cells,
                lax.ppermute(head, axis, [((i + 1) % count, i) for i in range(ends)]),
            ],
            axis=dim,
        )
    return cells


def per_device(
    jumps,
    base_aperture,
    pressure,
    block_fracture,
    send_face,
    elem_source,
    pair_local,
    send_block,
    tiles,
):
    nfrac_size = lax.axis_size("frac")
    blocks_here = jumps.shape[1]
    width = jumps.shape[2]
    vectors = pressure.shape[0]
    slot_count = pair_local.shape[0]
    padded_faces = jnp.concatenate([jumps, jnp.zeros((3, 1, width), jnp.float32)], axis=1)
    outgoing = padded_faces[:, send_face, :]
    incoming = lax.all_to_all(outgoing, "rock", split_axis=1, concat_axis=1, tiled=True)
    picked = incoming[:, elem_source, :]
    aperture = (
        base_aperture
        + 0.5 * jax.nn.softplus(picked[0])
        + 0.2 * (jnp.sqrt(1.0 + picked[1] ** 2 + picked[2] ** 2) - 1.0)
    )
    trans = aperture**3 / 12.0
    image = aperture[None] * pressure
    fracture = (
        jnp.broadcast_to(block_fracture[:, None], (blocks_here, width))
        .reshape(1, -1)
        .astype(jnp.float32)
    )
    stacked = jnp.concatenate(
        [pressure.reshape(vectors, -1), trans.reshape(1, -1), fracture], axis=0
    )
    edges = jnp.concatenate([stacked[:, :1], stacked[:, -1:]], axis=1)
    rims = padded(edges, ((("rock", "frac"), 1),), 1)
    extended = jnp.concatenate([rims[:, :1], stacked, rims[:, 3:]], axis=1)
    left_side = extended[:, :-1]
    right_side = extended[:, 1:]
    joined = (left_side[vectors + 1] == right_side[vectors + 1]).astype(jnp.float32)
    left_trans = left_side[vectors]
    right_trans = right_side[vectors]
    half_trans = 2.0 * left_trans * right_trans / (left_trans + right_trans) * joined
    flux = half_trans[None] * (left_side[:vectors] - right_side[:vectors])
    chain = flux[:, 1:] - flux[:, :-1]
    image = image + chain.reshape(vectors, blocks_here, width)
    values = jnp.concatenate([pressure, trans[None]], axis=0)
    pad_column = jnp.concatenate(
        [jnp.zeros((vectors, 1, width), jnp.float32), jnp.ones((1, 1, width), jnp.float32)], axis=0
    )
    padded_values = jnp.concatenate([values, pad_column], axis=1)
    block_ids = jnp.arange(blocks_here + 1, dtype=jnp.int32)
    pick_far = (send_block[:, None] == block_ids[None, :]).astype(jnp.float32)
    pick_near = (pair_local[:, None] == block_ids[None, :]).astype(jnp.float32)
    per_peer = slot_count // nfrac_size
    served = jnp.einsum("sb,vbw->vsw", pick_far, padded_values, precision=lax.Precision.HIGHEST)
    outgoing_values = served.reshape(vectors + 1, nfrac_size, per_peer, width)
    far_values = lax.all_to_all(
        outgoing_values, "frac", split_axis=1, concat_axis=1, tiled=True
    ).reshape(vectors + 1, slot_count, width)
    near_values = jnp.einsum(
        "sb,vbw->vsw", pick_near, padded_values, precision=lax.Precision.HIGHEST
    )
    near_press = near_values[:vectors]
    far_press = far_values[:vectors]
    near_trans = near_values[vectors]
    far_trans = far_values[vectors]
    mask = (pair_local < blocks_here).astype(jnp.float32)
    weights = (
        tiles.astype(jnp.float32)
        * (
            2.0
            * near_trans[:, :, None]
            * far_trans[:, None, :]
            / (near_trans[:, :, None] + far_trans[:, None, :])
        )
        * mask[:, None, None]
    )
    low_weights = weights.astype(jnp.bfloat16)
    near_low = near_press.astype(jnp.bfloat16)
    far_low = far_press.astype(jnp.bfloat16)
    near_term = jnp.sum(weights, axis=2)[None] * near_press - jnp.einsum(
        "sab,vsb->vsa", low_weights, far_low, preferred_element_type=jnp.float32
    )
    far_term = jnp.sum(weights, axis=1)[None] * far_press - jnp.einsum(
        "sab,vsa->vsb", low_weights, near_low, preferred_element_type=jnp.float32
    )
    returned = lax.all_to_all(
        far_term.reshape(vectors, nfrac_size, per_peer, width),
        "frac",
        split_axis=1,
        concat_axis=1,
        tiled=True,
    ).reshape(vectors, slot_count, width)
    spread = jnp.concatenate([pick_near, pick_far], axis=0)
    terms = jnp.concatenate([near_term, returned], axis=1)
    total = jnp.einsum("sb,vsw->vbw", spread, terms, precision=lax.Precision.HIGHEST)
    image = image + total[:, :blocks_here]
    return (image, aperture)


def solution(mesh):
    return jax.shard_map(
        per_device,
        mesh=mesh,
        in_specs=(
            P(None, ("rock", "frac"), None),
            P(("rock", "frac"), None),
            P(None, ("rock", "frac"), None),
            P(("rock", "frac")),
            P(("rock", "frac")),
            P(("rock", "frac")),
            P(("rock", "frac")),
            P(("rock", "frac")),
            P(("rock", "frac"), None, None),
        ),
        out_specs=(P(None, ("rock", "frac"), None), P(("rock", "frac"), None)),
        check_vma=False,
    )
```

profile of v0, /device:TPU:0, one launch (start us, length us, event | category | flops | bytes accessed | tf_op | source)
XLA Modules:
  0.0 197.3 jit_solution(15192222155171068244)
XLA Ops:
  0.6 2.5 %copy.23 = f32[3,1024,128]{2,0,1:T(4,128)S(1)} copy(f32[3,1024,128]{2,1,0:T(8,128)} %param.9) | data formatting | bytes 3145728 | tf_op args[0]
  3.1 0.7 fusion.31
  3.8 0.4 concatenate.28
  4.2 15.3 %gather_fusion = f32[2048,3,128]{2,1,0:T(4,128)} fusion(f32[3,1025,128]{2,0,1:T(4,128)S(1)} %concatenate.28, s32[2048]{0:T(1024)S(1)} %fusion.31), kind=kCustom, calls=%fused_computation | custom fusion | bytes 6299648 | tf_op jit(solution)/shard_map/gather | solution.py:41
  19.6 5.2 %all-to-all-start = ((f32[3,2048,128]{2,0,1:T(4,128)}), f32[3,2048,128]{2,0,1:T(4,128)}, u32[]{:S(2)}, u32[]{:S(2)}) async-start(f32[3,2048,128]{2,0,1:T(4,128)} %bitcast.71), calls=%async_computation | async-start | bytes 8388608 | tf_op jit(solution)/shard_map/all_to_all | solution.py:42
  24.8 11.7 %copy.45 = f32[2,8,1024,128]{3,1,2,0:T(8,128)} copy(f32[2,8,1024,128]{3,2,1,0:T(8,128)} %bitcast.70) | data formatting | bytes 16777216
  36.5 0.1 iota_compare_fusion.1
  36.7 36.6 %all-to-all-done = f32[3,2048,128]{2,0,1:T(4,128)} async-done(((f32[3,2048,128]{2,0,1:T(4,128)}), f32[3,2048,128]{2,0,1:T(4,128)}, u32[]{:S(2)}, u32[]{:S(2)}) %all-to-all-start) | async-done | bytes 3145760 | tf_op jit(solution)/shard_map/all_to_all | solution.py:42
  73.4 5.7 %gather_fusion.1 = f32[1024,3,128]{2,1,0:T(4,128)S(1)} fusion(f32[3,2048,128]{2,0,1:T(4,128)} %all-to-all-done, s32[1024]{0:T(1024)S(1)} %fusion.32), kind=kCustom, calls=%fused_computation.1 | custom fusion | bytes 3149824 | tf_op jit(solution)/shard_map/gather | solution.py:43
  79.1 0.1 copy.46
  79.2 0.6 fusion.37
  79.9 7.8 %fusion.7 = f32[17,8,8,128]{3,2,1,0:T(8,128)S(1)} fusion(f32[17,1,128]{2,1,0:T(1,128)S(1)} %copy-done.6, f32[1,1024,128]{2,1,0:T(8,128)S(1)} %get-tuple-element.4, f32[16,1024,128]{2,1,0:T(8,128)} %param.11, s32[64]{0:T(128)S(1)} %copy-done.4), kind=kOutput, calls=%fused_computation.24 | convolution fusion | flops 1717473536 | bytes 9478912 | tf_op jit(solution)/shard_map/sb,vbw->vsw/dot_general | solution.py:80
  87.7 7.7 %fusion.6 = f32[17,64,128]{2,1,0:T(8,128)S(1)} fusion(f32[17,1,128]{2,1,0:T(1,128)S(1)} %copy-done.6, f32[1,1024,128]{2,1,0:T(8,128)S(1)} %get-tuple-element.4, f32[16,1024,128]{2,1,0:T(8,128)} %param.11, s32[64]{0:T(128)S(1)} %copy-done.5), kind=kOutput, calls=%fused_computation.23 | convolution fusion | flops 1717473536 | bytes 9478912 | tf_op jit(solution)/shard_map/sb,vbw->vsw/dot_general | solution.py:85
  95.6 0.2 broadcast_in_dim.10
  95.9 1.3 collective-permute-start.1
  97.1 3.0 %collective-permute-start = (f32[18,1]{1,0:T(8,128)S(1)}, f32[18,1]{1,0:T(8,128)S(1)}, u32[]{:S(2)}, u32[]{:S(2)}) collective-permute-start(f32[18,1]{1,0:T(8,128)S(1)} %get-tuple-element.6), channel_id=1, source_target_pairs={{0,1},{1,2},{2,3},{3,4},{4,5},{5,6},{6,7},{7,8},{8,9},{9,10},{10,1... | collective-permute-start | bytes 224 | tf_op jit(solution)/shard_map/ppermute | solution.py:15
  100.2 0.8 copy.27
  101.0 7.7 %all-to-all-start.1 = ((f32[17,8,8,128]{3,2,0,1:T(8,128)}), f32[17,8,8,128]{3,2,0,1:T(8,128)S(1)}, u32[]{:S(2)}, u32[]{:S(2)}) async-start(f32[17,8,8,128]{3,2,0,1:T(8,128)} %copy.27), calls=%async_computation.1 | async-start | bytes 1114112 | tf_op jit(solution)/shard_map/all_to_all | solution.py:82
  108.7 10.2 %fusion.19 = f32[131073]{0:T(1024)S(1)} fusion(f32[18,1]{1,0:T(8,128)S(1)} %collective-permute-done.1, f32[1,131072]{1,0:T(1,128)S(1)} %bitcast.76, f32[1,131072]{1,0:T(1,128)S(1)} %bitcast.73, f32[16,131072]{1,0:T(8,128)} %bitcast.65, f32[18,1]{1,0:T(8,128)S(1)} %collective-permute-done), kind=kLoop, calls=%fused_computation.41 | loop fusion | flops 2359314 | bytes 9961620 | tf_op jit(solution)/shard_map/mul | solution.py:67
  118.9 12.1 %fusion.1 = f32[16,131073]{1,0:T(8,128)} fusion(f32[18,1]{1,0:T(8,128)S(1)} %collective-permute-done.1, f32[1,131072]{1,0:T(1,128)S(1)} %bitcast.77, f32[1,131072]{1,0:T(1,128)S(1)} %bitcast.74, f32[16,131072]{1,0:T(8,128)} %bitcast.66, f32[18,1]{1,0:T(8,128)S(1)} %collective-permute-done, f32[131073]{0:T(1024)S(1)} %fusion.19), kind=kLoop, calls=%fused_computation.5 | loop fusion | flops 16777344 | bytes 18350292 | tf_op jit(solution)/shard_map/mul | solution.py:68
  130.9 11.4 %fusion.3 = f32[2,8,1024,128]{3,1,2,0:T(8,128)} fusion(f32[16,131073]{1,0:T(8,128)} %fusion.1), kind=kLoop, calls=%fused_computation.15 | loop fusion | flops 2097152 | bytes 25165824
  142.4 8.3 %copy.38 = f32[2,8,1024,128]{3,2,1,0:T(8,128)} copy(f32[2,8,1024,128]{3,1,2,0:T(8,128)} %fusion.3) | data formatting | bytes 16777216
  150.7 0.1 copy.28
  150.8 5.0 %fusion.39 = (f32[64,128]{1,0:T(8,128)S(1)}, f32[64,128]{1,0:T(8,128)S(1)}) fusion(f32[64]{0:T(128)S(1)} %compare_convert_fusion, f32[64,128]{1,0:T(8,128)S(1)} %slice_bitcast_fusion.2, f32[64,128]{1,0:T(8,128)S(1)} %slice_bitcast_fusion.1, f32[64,128]{1,0:T(8,128)S(1)} %broadcast_multiply_fusion, bf16[64,128,128]{2,1,0:T(8,128)(2,1)} %param.17), kind=kLoop, calls=%fused_computation.80 | loop fusion | flops 8372224 | bytes 2261248 | tf_op jit(solution)/shard_map/reduce_sum | solution.py:106
  155.9 6.2 %fusion.8 = f32[16,64,128]{2,0,1:T(8,128)S(1)} fusion(f32[16,64,128]{2,0,1:T(8,128)S(1)} %bitcast_multiply_fusion, bf16[16,64,128]{2,1,0:T(8,128)(2,1)S(1)} %slice.129, bf16[64,128,128]{2,1,0:T(8,128)(2,1)} %param.17, f32[64]{0:T(128)S(1)} %compare_convert_fusion, f32[64,128]{1,0:T(8,128)S(1)} %slice_bitcast_fusion.2, ...), kind=kOutput, calls=%fused_computation.26 | convolution fusion | flops 41025536 | bytes 3506432 | tf_op jit(solution)/shard_map/sab,vsa->vsb/dot_general | solution.py:109
  162.1 1.0 copy.31
  163.1 5.1 %all-to-all-start.2 = ((f32[16,8,8,128]{3,2,0,1:T(8,128)}), f32[16,8,8,128]{3,2,0,1:T(8,128)S(1)}, u32[]{:S(2)}, u32[]{:S(2)}) async-start(f32[16,8,8,128]{3,2,0,1:T(8,128)} %copy.31), calls=%async_computation.2 | async-start | bytes 1048576 | tf_op jit(solution)/shard_map/all_to_all | solution.py:112
  168.2 4.4 %fusion.13 = f32[64,16,128]{2,1,0:T(8,128)S(1)} fusion(bf16[16,64,128]{2,0,1:T(8,128)(2,1)S(1)} %bitcast_convert_fusion, bf16[64,128,128]{2,1,0:T(8,128)(2,1)} %param.17, f32[64]{0:T(128)S(1)} %compare_convert_fusion, f32[64,128]{1,0:T(8,128)S(1)} %slice_bitcast_fusion.2, f32[64,128]{1,0:T(8,128)S(1)} %slice_bitcast_fusion.1, ...), kind=kOutput, calls=%fused_computation.31 | convolution fusion | flops 40894464 | bytes 2982144 | tf_op jit(solution)/shard_map/sab,vsb->vsa/dot_general | solution.py:106
  172.5 0.2 bitcast_subtract_fusion
  172.7 10.8 %all-to-all-done.2 = f32[16,8,8,128]{3,2,0,1:T(8,128)S(1)} async-done(((f32[16,8,8,128]{3,2,0,1:T(8,128)}), f32[16,8,8,128]{3,2,0,1:T(8,128)S(1)}, u32[]{:S(2)}, u32[]{:S(2)}) %all-to-all-start.2) | async-done | bytes 524320 | tf_op jit(solution)/shard_map/all_to_all | solution.py:112
  183.5 3.6 %convolution_bitcast_fusion = f32[16,1025,128]{2,1,0:T(8,128)S(1)} fusion(f32[16,64,128]{2,1,0:T(8,128)S(1)} %bitcast.79, f32[16,64,128]{2,1,0:T(8,128)S(1)} %bitcast_subtract_fusion, pred[64,1025]{0,1:T(8,128)(4,1)S(1)} %iota_compare_fusion, pred[64,1025]{0,1:T(8,128)(4,1)S(1)} %iota_compare_fusion.1), kind=kOutput, calls=%fused_computation.16 | convolution fusion | flops 3224764416 | bytes 9576576 | tf_op jit(solution)/shard_map/sb,vsw->vbw/dot_general | solution.py:121
  187.2 10.1 %fusion.2 = f32[16,1024,128]{2,1,0:T(8,128)} fusion(f32[2,8,1024,128]{3,2,1,0:T(8,128)} %copy.38, f32[16,1025,128]{2,1,0:T(8,128)S(1)} %convolution_bitcast_fusion, f32[16,1024,128]{2,1,0:T(8,128)} %param.11, f32[1024,128]{1,0:T(8,128)S(1)} %get-tuple-element.5), kind=kLoop, calls=%fused_computation.12 | loop fusion | flops 6291456 | bytes 34078720 | tf_op jit(solution)/shard_map/add | solution.py:122
  (36 shorter events, 0.5 us)
Async XLA Ops:
  4.2 20.5 %copy-start.2 = (s32[1024]{0:T(1024)S(1)}, s32[1024]{0:T(1024)}, u32[]{:S(2)}) copy-start(s32[1024]{0:T(1024)} %param.12) | copy-start | bytes 12292
  19.6 53.8 %all-to-all-start = ((f32[3,2048,128]{2,0,1:T(4,128)}), f32[3,2048,128]{2,0,1:T(4,128)}, u32[]{:S(2)}, u32[]{:S(2)}) async-start(f32[3,2048,128]{2,0,1:T(4,128)} %bitcast.71), calls=%async_computation | async-start | bytes 8388608 | tf_op jit(solution)/shard_map/all_to_all | solution.py:42
  24.8 11.7 %copy-start.5 = (s32[64]{0:T(128)S(1)}, s32[64]{0:T(128)}, u32[]{:S(2)}) copy-start(s32[64]{0:T(128)} %param.15) | copy-start | bytes 772
  24.8 11.7 %copy-start.3 = (s32[1024]{0:T(1024)S(1)}, s32[1024]{0:T(1024)}, u32[]{:S(2)}) copy-start(s32[1024]{0:T(1024)} %param.14) | copy-start | bytes 12292
  24.8 11.9 %copy-start.4 = (s32[64]{0:T(128)S(1)}, s32[64]{0:T(128)}, u32[]{:S(2)}) copy-start(s32[64]{0:T(128)} %param.16) | copy-start | bytes 772
  24.8 54.4 %copy-start.1 = (f32[1024,128]{1,0:T(8,128)S(1)}, f32[1024,128]{1,0:T(8,128)}, u32[]{:S(2)}) copy-start(f32[1024,128]{1,0:T(8,128)} %param.10) | copy-start | bytes 1572868
  36.5 43.3 %copy-start.6 = (f32[17,1,128]{2,1,0:T(1,128)S(1)}, f32[17,1,128]{2,1,0:T(1,128)}, u32[]{:S(2)}) copy-start(f32[17,1,128]{2,1,0:T(1,128)} %constant.11.clone.1) | copy-start | bytes 26116
  79.8 107.4 %copy-start = (f32[1024,128]{1,0:T(8,128)}, f32[1024,128]{1,0:T(8,128)S(1)}, u32[]{:S(2)}) copy-start(f32[1024,128]{1,0:T(8,128)S(1)} %get-tuple-element.5) | copy-start | bytes 1572868
  79.8 15.9 %slice-start = ((s8[8388608]{0:T(1024)(128)(4,1)}), s8[4194304]{0:T(1024)(128)(4,1)S(1)}, s32[]{:S(2)}) async-start(s8[8388608]{0:T(1024)(128)(4,1)} %bitcast.67), calls=%async_computation.3 | async-start | bytes 8388608
  87.7 8.1 %slice-start.1 = ((s8[8388608]{0:T(1024)(128)(4,1)}), s8[4194304]{0:T(1024)(128)(4,1)S(1)}, s32[]{:S(2)}) async-start(s8[8388608]{0:T(1024)(128)(4,1)} %bitcast.67), calls=%async_computation.4 | async-start | bytes 8388608
  95.9 12.9 %collective-permute-start.1 = (f32[18,1]{1,0:T(8,128)S(1)}, f32[18,1]{1,0:T(8,128)S(1)}, u32[]{:S(2)}, u32[]{:S(2)}) collective-permute-start(f32[18,1]{1,0:T(8,128)S(1)} %get-tuple-element.7), channel_id=1, source_target_pairs={{1,0},{2,1},{3,2},{4,3},{5,4},{6,5},{7,6},{8,7},{9,8},{10,9},{11,1... | collective-permute-start | bytes 224 | tf_op jit(solution)/shard_map/ppermute | solution.py:17
  97.1 11.6 %collective-permute-start = (f32[18,1]{1,0:T(8,128)S(1)}, f32[18,1]{1,0:T(8,128)S(1)}, u32[]{:S(2)}, u32[]{:S(2)}) collective-permute-start(f32[18,1]{1,0:T(8,128)S(1)} %get-tuple-element.6), channel_id=1, source_target_pairs={{0,1},{1,2},{2,3},{3,4},{4,5},{5,6},{6,7},{7,8},{8,9},{9,10},{10,1... | collective-permute-start | bytes 224 | tf_op jit(solution)/shard_map/ppermute | solution.py:15
  101.0 49.6 %all-to-all-start.1 = ((f32[17,8,8,128]{3,2,0,1:T(8,128)}), f32[17,8,8,128]{3,2,0,1:T(8,128)S(1)}, u32[]{:S(2)}, u32[]{:S(2)}) async-start(f32[17,8,8,128]{3,2,0,1:T(8,128)} %copy.27), calls=%async_computation.1 | async-start | bytes 1114112 | tf_op jit(solution)/shard_map/all_to_all | solution.py:82
  163.1 20.4 %all-to-all-start.2 = ((f32[16,8,8,128]{3,2,0,1:T(8,128)}), f32[16,8,8,128]{3,2,0,1:T(8,128)S(1)}, u32[]{:S(2)}, u32[]{:S(2)}) async-start(f32[16,8,8,128]{3,2,0,1:T(8,128)} %copy.31), calls=%async_computation.2 | async-start | bytes 1048576 | tf_op jit(solution)/shard_map/all_to_all | solution.py:112
where the time goes:
time: 198 us; the launch traced here: 197 us
  other arithmetic  50.7 us (26%)
  waiting for transfers between devices  47.4 us (24%)
  local copies, waits for them, and re-layouts  46.3 us (23%)
  matrix products  29.8 us (15%)
  starting transfers between devices  22.3 us (11%)
    all_to_all x1, waiting for transfers between devices, per_device(): lax.all_to_all(outgoing, 'rock', split_axis=1, concat_axis=1, tiled=True)  36.6 us
    unnamed x21, local copies, waits for them, and re-layouts  22.5 us
    gather x1, local copies, waits for them, and re-layouts, per_device(): outgoing = padded_faces[:, send_face, :]  15.3 us
    mul x1, other arithmetic, per_device(): flux = half_trans[None] * (left_side[:vectors] - right_side[:vectors])  12.1 us
    unnamed x2, other arithmetic  11.4 us
    all_to_all x1, waiting for transfers between devices, per_device(): lax.all_to_all(far_term.reshape(vectors, nfrac_size, per_peer, width), 'f...  10.8 us
    mul x1, other arithmetic, per_device(): 2.0 * left_trans * right_trans / (left_trans + right_trans) * joined  10.2 us
    add x1, other arithmetic, per_device(): image = image + total[:, :blocks_here]  10.1 us
  transfers between devices with their start and end apart: 5, of which 2 were waited for; matrix products, arithmetic and copies ran while one was open for 30% of the time, Pallas kernels for 0%

commit v1 on v0

v1 whole, which is shorter than its diff:
```python
import functools

import jax
import jax.numpy as jnp
from jax import lax
from jax.experimental import pallas as pl
from jax.experimental.pallas import tpu as pltpu
from jax.sharding import PartitionSpec as P

MESH = pl.DeviceIdType.MESH
F32 = jnp.float32
BF16 = jnp.bfloat16
LANES = 128
VMEM_LIMIT = 60 * 1024 * 1024


def split(x):
    hi = x.astype(BF16)
    return hi, (x - hi.astype(F32)).astype(BF16)


def split_lanes(x):
    return jnp.concatenate(split(x), axis=1)


def fold(x):
    half = x.shape[1] // 2
    return x[:, :half] + x[:, half:]


def column(row):
    return jnp.broadcast_to(row, (LANES, LANES)).T


def one_hot(col, width):
    lane = lax.broadcasted_iota(jnp.int32, (LANES, LANES), 1)
    parts = [
        jnp.where(col == lane + k * LANES, 1.0, 0.0).astype(BF16) for k in range(width // LANES)
    ]
    return jnp.concatenate(parts, axis=1)


def dot(a, b):
    return jnp.dot(a, b, preferred_element_type=F32)


def dot_nt(a, b):
    return lax.dot_general(a, b, (((1,), (1,)), ((), ())), preferred_element_type=F32)


def exchange_kernel(
    nr,
    nf,
    jumps_hbm,
    base_hbm,
    press_hbm,
    tiles_hbm,
    face_ref,
    elem_ref,
    slot_ref,
    frac_ref,
    ap_ref,
    terms_ref,
    left_ref,
    right_ref,
    jumps,
    base,
    press,
    tiles,
    gap,
    face_out,
    face_in,
    elem_hot,
    pair_hot,
    acc,
    near_p,
    far_out,
    far_in,
    near_t,
    trans_out,
    trans_in,
    near_term,
    ret_out,
    ret_in,
    edge_out,
    load_sem,
    face_ss,
    face_rs,
    far_ss,
    far_rs,
    trans_ss,
    trans_rs,
    ret_ss,
    ret_rs,
    edge_ss,
    edge_rs,
):
    me_r = lax.axis_index("rock")
    me_f = lax.axis_index("frac")
    nv, eb, width = press.shape
    cap = far_in.shape[2]
    slots = nf * cap
    capf = face_in.shape[1]
    nsub = capf // LANES
    count = nr * nf
    me = me_r * nf + me_f
    after = lax.rem(me + 1, count)
    before = lax.rem(me + count - 1, count)
    after_id = (after // nf, lax.rem(after, nf))
    before_id = (before // nf, lax.rem(before, nf))

    loads = [
        pltpu.make_async_copy(src, dst, load_sem.at[i])
        for i, (src, dst) in enumerate(
            [(jumps_hbm, jumps), (base_hbm, base), (press_hbm, press), (tiles_hbm, tiles)]
        )
    ]
    for load in loads:
        load.start()

    barrier = pltpu.get_barrier_semaphore()
    for d in range(1, nr):
        peer = lax.rem(me_r + d, nr)
        pl.semaphore_signal(barrier, inc=1, device_id={"rock": peer}, device_id_type=MESH)
    for d in range(1, nf):
        peer = lax.rem(me_f + d, nf)
        pl.semaphore_signal(barrier, inc=1, device_id={"frac": peer}, device_id_type=MESH)
    for ident in (after_id, before_id):
        pl.semaphore_signal(barrier, inc=1, device_id=ident, device_id_type=MESH)

    loads[0].wait()

    def gap_step(k, _):
        rows = pl.ds(pl.multiple_of(k * LANES, LANES), LANES)
        a, b, c = jumps[0, rows, :], jumps[1, rows, :], jumps[2, rows, :]
        soft = jnp.maximum(a, 0.0) + jnp.log1p(jnp.exp(-jnp.abs(a)))
        gap[rows, :] = split_lanes(0.5 * soft + 0.2 * (jnp.sqrt(1.0 + b * b + c * c) - 1.0))
        return 0

    lax.fori_loop(0, eb // LANES, gap_step, 0)

    def face_rows(peer, m):
        row = face_ref[pl.ds(peer * nsub + m, 1), :]
        return fold(dot(one_hot(column(row), eb), gap[...]))

    def sub(m):
        return pl.ds(pl.multiple_of(m * LANES, LANES), LANES)

    def face_copy(peer, m, slot):
        return pltpu.make_async_remote_copy(
            src_ref=face_out.at[peer, sub(m)],
            dst_ref=face_in.at[slot, sub(m)],
            send_sem=face_ss.at[peer, m],
            recv_sem=face_rs.at[slot, m],
            device_id={"rock": peer},
            device_id_type=MESH,
        )

    pl.semaphore_wait(barrier, nr - 1 + nf - 1 + 2)

    def face_step(k, _):
        peer = lax.rem(me_r + 1 + k // nsub, nr)
        m = lax.rem(k, nsub)
        face_out[peer, sub(m), :] = face_rows(peer, m)
        face_copy(peer, m, me_r).start()
        return 0

    lax.fori_loop(0, (nr - 1) * nsub, face_step, 0)

    for g in range(2 * slots // LANES):
        pair_hot[g * LANES : (g + 1) * LANES, :] = one_hot(
            column(slot_ref[:, g * LANES : (g + 1) * LANES]), eb
        )
    loads[2].wait()

    def press_step(v, _):
        picked = fold(dot(pair_hot[...], split_lanes(press[v])))
        near_p[:, v] = picked[:slots].reshape(nf, cap, width)
        far_out[:, v] = picked[slots:].reshape(nf, cap, width)
        return 0

    lax.fori_loop(0, nv, press_step, 0)

    def far_copy(peer, slot):
        return pltpu.make_async_remote_copy(
            src_ref=far_out.at[peer],
            dst_ref=far_in.at[slot],
            send_sem=far_ss.at[peer],
            recv_sem=far_rs.at[slot],
            device_id={"frac": peer},
            device_id_type=MESH,
        )

    for d in range(1, nf):
        far_copy(lax.rem(me_f + d, nf), me_f).start()
    far_in[me_f] = far_out[me_f]

    def own_step(m, _):
        face_in[me_r, sub(m), :] = face_rows(me_r, m)
        return 0

    lax.fori_loop(0, nsub, own_step, 0)

    def elem_step(k, _):
        col = column(elem_ref[pl.ds(k, 1), :])
        for s in range(nr):
            elem_hot[s, sub(k), :] = one_hot(col - s * capf, capf)
        return 0

    lax.fori_loop(0, eb // LANES, elem_step, 0)

    loads[1].wait()
    acc[...] = base[...]

    def take(s):
        faces = split_lanes(face_in[s])

        def step(k, _):
            acc[sub(k), :] += fold(dot(elem_hot[s, sub(k), :], faces))
            return 0

        lax.fori_loop(0, eb // LANES, step, 0)

    take(me_r)
    for d in range(1, nr):
        source = lax.rem(me_r + nr - d, nr)
        for m in range(nsub):
            face_copy(source, m, source).wait_recv()
        take(source)

    aperture = acc[...]
    ap_ref[...] = aperture
    trans = aperture * aperture * aperture / 12.0

    picked_t = fold(dot(pair_hot[...], split_lanes(trans)))
    picked_t = jnp.where(picked_t == 0.0, 1.0, picked_t)
    near_t[...] = picked_t[:slots].reshape(nf, cap, width)
    trans_out[...] = picked_t[slots:].reshape(nf, cap, width)

    def trans_copy(peer, slot):
        return pltpu.make_async_remote_copy(
            src_ref=trans_out.at[peer],
            dst_ref=trans_in.at[slot],
            send_sem=trans_ss.at[peer],
            recv_sem=trans_rs.at[slot],
            device_id={"frac": peer},
            device_id_type=MESH,
        )

    for d in range(1, nf):
        trans_copy(lax.rem(me_f + d, nf), me_f).start()
    trans_in[me_f] = trans_out[me_f]

    for side, at in ((0, eb - 1), (1, 0)):
        for v in range(nv):
            edge_out[side, v : v + 1, :] = press[v, at : at + 1, :]
        edge_out[side, nv : nv + 1, :] = trans[at : at + 1, :]
        edge_out[side, nv + 1 : nv + 2, :] = jnp.broadcast_to(
            frac_ref[at // width : at // width + 1, at % width : at % width + 1], (1, width)
        ).astype(F32)
        edge_out[side, nv + 2 :, :] = jnp.zeros((edge_out.shape[1] - nv - 2, width), F32)

    edges = [
        pltpu.make_async_remote_copy(
            src_ref=edge_out.at[side],
            dst_ref=dst,
            send_sem=edge_ss.at[side],
            recv_sem=edge_rs.at[side],
            device_id=ident,
            device_id_type=MESH,
        )
        for side, dst, ident in ((0, left_ref, after_id), (1, right_ref, before_id))
    ]
    for edge in edges:
        edge.start()

    def ret_copy(peer, slot):
        return pltpu.make_async_remote_copy(
            src_ref=ret_out.at[peer],
            dst_ref=ret_in.at[slot],
            send_sem=ret_ss.at[peer],
            recv_sem=ret_rs.at[slot],
            device_id={"frac": peer},
            device_id_type=MESH,
        )

    loads[3].wait()
    ones = jnp.ones((nv, 2 * width), BF16)
    none = jnp.zeros((nv, width), BF16)

    def terms_of(q):
        near_tr = jnp.concatenate(
            [near_t[q], jnp.ones((LANES - cap, width), F32)], axis=0
        ).T
        far_tr = trans_in[q]
        for c in range(cap):
            n = near_tr[:, c : c + 1]
            f = far_tr[c : c + 1, :]
            w = tiles[q * cap + c].astype(F32) * (2.0 * n * f / (n + f))
            hi, lo = split(w)
            pn = near_p[q, :, c, :]
            pf = far_in[q, :, c, :]
            left = jnp.concatenate(
                [jnp.concatenate([pf.astype(BF16), none], axis=1), ones], axis=0
            )
            both = dot_nt(left, jnp.concatenate([hi, lo], axis=1))
            near_term[q, :, c, :] = both[nv:] * pn - both[:nv]
            ret_out[q, :, c, :] = jnp.sum(w, axis=0, keepdims=True) * pf - dot(
                pn.astype(BF16), hi
            )

    def terms_step(d, _):
        q = lax.rem(me_f + nf - d, nf)
        trans_copy(q, q).wait_recv()
        far_copy(q, q).wait_recv()
        terms_of(q)
        ret_copy(q, me_f).start()
        return 0

    lax.fori_loop(1, nf, terms_step, 0)
    terms_of(me_f)
    ret_in[me_f] = ret_out[me_f]

    for v in range(nv):
        hi, lo = split(near_term[:, v].reshape(slots, width))
        terms_ref[v, :slots, :] = hi
        terms_ref[v, 2 * slots : 3 * slots, :] = lo

    for d in range(1, nf):
        q = lax.rem(me_f + nf - d, nf)
        ret_copy(q, q).wait_recv()

    for v in range(nv):
        hi, lo = split(ret_in[:, v].reshape(slots, width))
        terms_ref[v, slots : 2 * slots, :] = hi
        terms_ref[v, 3 * slots :, :] = lo

    for edge in edges:
        edge.wait()
    for d in range(1, nr):
        peer = lax.rem(me_r + d, nr)
        for m in range(nsub):
            face_copy(peer, m, me_r).wait_send()
    for d in range(1, nf):
        peer = lax.rem(me_f + d, nf)
        far_copy(peer, me_f).wait_send()
        trans_copy(peer, me_f).wait_send()
        ret_copy(peer, me_f).wait_send()


def harmonic(a, b):
    return 2.0 * a * b / (a + b)


def image_kernel(
    count,
    p_ref,
    pl_ref,
    pr_ref,
    a_ref,
    al_ref,
    ar_ref,
    frac_ref,
    left_ref,
    right_ref,
    slot_ref,
    terms_ref,
    out_ref,
    ap_ref,
):
    nv, rows, width = p_ref.shape
    halo = pl_ref.shape[1]
    i = pl.program_id(0)
    n = pl.num_programs(0)
    first = i == 0
    last = i == n - 1
    me = lax.axis_index("rock") * lax.axis_size("frac") + lax.axis_index("frac")
    has_left = jnp.where(first & (me == 0), 0.0, 1.0)
    has_right = jnp.where(last & (me == count - 1), 0.0, 1.0)
    lane = lax.broadcasted_iota(jnp.int32, (rows, width), 1)
    row = lax.broadcasted_iota(jnp.int32, (rows, width), 0)
    first_lane, last_lane = lane == 0, lane == width - 1
    first_row, last_row = row == 0, row == rows - 1

    def up(x, nxt):
        below = jnp.where(last_row, nxt, pltpu.roll(x, rows - 1, 0))
        return pltpu.roll(jnp.where(first_lane, below, x), width - 1, 1)

    def down(x, prv):
        above = jnp.where(first_row, prv, pltpu.roll(x, 1, 0))
        return pltpu.roll(jnp.where(last_lane, above, x), 1, 1)

    a = a_ref[...]
    ap_ref[...] = a

    def tr(x):
        return x * x * x / 12.0

    t = tr(a)
    t_prv = jnp.where(first, left_ref[nv : nv + 1, :], tr(al_ref[halo - 1 :, :]))
    t_nxt = jnp.where(last, right_ref[nv : nv + 1, :], tr(ar_ref[:1, :]))

    fr_row = frac_ref[pl.ds(i, 1), :].astype(F32)
    fr = jnp.broadcast_to(fr_row, (rows, width)).T
    fr_left = frac_ref[pl.ds(jnp.maximum(i - 1, 0), 1), :].astype(F32)[:, width - 1 :]
    fr_right = frac_ref[pl.ds(jnp.minimum(i + 1, n - 1), 1), :].astype(F32)[:, :1]
    fr_prv = jnp.where(first, left_ref[nv + 1 : nv + 2, :1], fr_left)
    fr_nxt = jnp.where(last, right_ref[nv + 1 : nv + 2, :1], fr_right)
    fr_below = jnp.where(last_row, fr_nxt, pltpu.roll(fr, rows - 1, 0))
    joined = jnp.where(last_row & last_lane, has_right, 1.0) * jnp.where(
        last_lane & (fr_below != fr), 0.0, 1.0
    )
    h = harmonic(t, up(t, t_nxt)) * joined
    joined_prv = jnp.where(fr_prv == fr[:1, :], 1.0, 0.0) * has_left
    h_prv = harmonic(t_prv, pltpu.roll(t[:8], width - 1, 1)[:1]) * joined_prv

    ids = i * rows + lax.broadcasted_iota(jnp.int32, (rows, slot_ref.shape[1]), 0)
    hot = jnp.where(ids == slot_ref[...], 1.0, 0.0).astype(BF16)

    for v in range(nv):
        p = p_ref[v]
        p_prv = jnp.where(first, left_ref[v : v + 1, :], pl_ref[v, halo - 1 :, :])
        p_nxt = jnp.where(last, right_ref[v : v + 1, :], pr_ref[v, :1, :])
        flux = h * (p - up(p, p_nxt))
        flux_prv = h_prv * (p_prv - pltpu.roll(p[:8], width - 1, 1)[:1])
        out_ref[v] = a * p + flux - down(flux, flux_prv) + dot(hot, terms_ref[v])


def per_device(
    jumps,
    base_aperture,
    pressure,
    block_fracture,
    send_face,
    elem_source,
    pair_local,
    send_block,
    tiles,
):
    nr, nf = lax.axis_size("rock"), lax.axis_size("frac")
    nv, eb, width = pressure.shape
    slots = pair_local.shape[0]
    cap = slots // nf
    capf = send_face.shape[0] // nr
    nsub = capf // LANES
    edge_rows = -(-(nv + 2) // 8) * 8
    frac = block_fracture.reshape(eb // LANES, LANES)
    slot_row = jnp.concatenate([pair_local, send_block, pair_local, send_block]).reshape(1, -1)
    any_spec = pl.BlockSpec(memory_space=pl.ANY)
    vmem = pl.BlockSpec(memory_space=pltpu.VMEM)
    dma = pltpu.SemaphoreType.DMA
    peers = (nf, nv, cap, width)
    aperture, terms, left, right = pl.pallas_call(
        functools.partial(exchange_kernel, nr, nf),
        out_shape=(
            jax.ShapeDtypeStruct((eb, width), F32),
            jax.ShapeDtypeStruct((nv, 4 * slots, width), BF16),
            jax.ShapeDtypeStruct((edge_rows, width), F32),
            jax.ShapeDtypeStruct((edge_rows, width), F32),
        ),
        in_specs=[any_spec] * 4 + [vmem] * 4,
        out_specs=(vmem,) * 4,
        scratch_shapes=[
            pltpu.VMEM((3, eb, width), F32),
            pltpu.VMEM((eb, width), F32),
            pltpu.VMEM((nv, eb, width), F32),
            pltpu.VMEM((slots, width, width), BF16),
            pltpu.VMEM((eb, 2 * width), BF16),
            pltpu.VMEM((nr, capf, width), F32),
            pltpu.VMEM((nr, capf, width), F32),
            pltpu.VMEM((nr, eb, capf), BF16),
            pltpu.VMEM((2 * slots, eb), BF16),
            pltpu.VMEM((eb, width), F32),
            pltpu.VMEM(peers, F32),
            pltpu.VMEM(peers, F32),
            pltpu.VMEM(peers, F32),
            pltpu.VMEM((nf, cap, width), F32),
            pltpu.VMEM((nf, cap, width), F32),
            pltpu.VMEM((nf, cap, width), F32),
            pltpu.VMEM(peers, F32),
            pltpu.VMEM(peers, F32),
            pltpu.VMEM(peers, F32),
            pltpu.VMEM((2, edge_rows, width), F32),
            dma((4,)),
            dma((nr, nsub)),
            dma((nr, nsub)),
            dma((nf,)),
            dma((nf,)),
            dma((nf,)),
            dma((nf,)),
            dma((nf,)),
            dma((nf,)),
            dma((2,)),
            dma((2,)),
        ],
        compiler_params=pltpu.CompilerParams(
            collective_id=0, has_side_effects=True, vmem_limit_bytes=VMEM_LIMIT
        ),
        name="exchange",
    )(
        jumps,
        base_aperture,
        pressure,
        tiles,
        send_face.reshape(-1, LANES),
        elem_source.reshape(-1, LANES),
        slot_row,
        frac,
    )
    rows = LANES
    halo = 8
    step = rows // halo
    end = eb // halo - 1
    before = lambda i: jnp.maximum(i * step - 1, 0)
    after = lambda i: jnp.minimum((i + 1) * step, end)
    return pl.pallas_call(
        functools.partial(image_kernel, nr * nf),
        grid=(eb // rows,),
        out_shape=(
            jax.ShapeDtypeStruct((nv, eb, width), F32),
            jax.ShapeDtypeStruct((eb, width), F32),
        ),
        in_specs=[
            pl.BlockSpec((nv, rows, width), lambda i: (0, i, 0)),
            pl.BlockSpec((nv, halo, width), lambda i: (0, before(i), 0)),
            pl.BlockSpec((nv, halo, width), lambda i: (0, after(i), 0)),
            pl.BlockSpec((rows, width), lambda i: (i, 0)),
            pl.BlockSpec((halo, width), lambda i: (before(i), 0)),
            pl.BlockSpec((halo, width), lambda i: (after(i), 0)),
            vmem,
            vmem,
            vmem,
            vmem,
            vmem,
        ],
        out_specs=(
            pl.BlockSpec((nv, rows, width), lambda i: (0, i, 0)),
            pl.BlockSpec((rows, width), lambda i: (i, 0)),
        ),
        compiler_params=pltpu.CompilerParams(vmem_limit_bytes=VMEM_LIMIT),
        name="image",
    )(
        pressure,
        pressure,
        pressure,
        aperture,
        aperture,
        aperture,
        frac,
        left,
        right,
        slot_row,
        terms,
    )


def solution(mesh):
    split_axes = ("rock", "frac")
    return jax.shard_map(
        per_device,
        mesh=mesh,
        in_specs=(
            P(None, split_axes, None),
            P(split_axes, None),
            P(None, split_axes, None),
            P(split_axes),
            P(split_axes),
            P(split_axes),
            P(split_axes),
            P(split_axes),
            P(split_axes, None, None),
        ),
        out_specs=(P(None, split_axes, None), P(split_axes, None)),
        check_vma=False,
    )
```

time: 198 us -> 61.1 us (0.31)
  Pallas kernels: 0 us -> 58.8 us
  other arithmetic: 50.7 us -> 1.39 us
  waiting for transfers between devices: 47.4 us -> 0 us
  local copies, waits for them, and re-layouts: 46.3 us -> 0 us
  matrix products: 29.8 us -> 0 us
  starting transfers between devices: 22.3 us -> 0 us
    pallas_call x0 -> x2, Pallas kernels: none -> 58.8 us  [the longest x1 42.2 us: per_device(): pl.pallas_call(functools.partial(exchange_kernel, nr, nf), out_shape=(jax...]
    all_to_all x3 -> x0, waiting for transfers between devices: 47.4 us -> none  [the longest x1 36.6 us: per_device(): lax.all_to_all(outgoing, 'rock', split_axis=1, concat_axis=1, tiled=True)]
    dot_general x5 -> x0, matrix products: 29.8 us -> none  [the longest x1 7.8 us: per_device(): jnp.einsum('sb,vbw->vsw', pick_far, padded_values, precision=lax.Precisio...]
    unnamed x21 -> x0, local copies, waits for them, and re-layouts: 22.5 us -> none
    mul x4 -> x0, other arithmetic: 22.3 us -> none  [the longest x1 12.1 us: per_device(): flux = half_trans[None] * (left_side[:vectors] - right_side[:vectors])]
    gather x3 -> x0, local copies, waits for them, and re-layouts: 21.1 us -> none  [the longest x1 15.3 us: per_device(): outgoing = padded_faces[:, send_face, :]]
    all_to_all x3 -> x0, starting transfers between devices: 18 us -> none  [the longest x1 7.69 us: per_device(): lax.all_to_all(outgoing_values, 'frac', split_axis=1, concat_axis=1, tile...]
    unnamed x2 -> x0, other arithmetic: 11.4 us -> none
  transfers between devices with their start and end apart: 5 -> 0, of which waited for: 2 -> 0; matrix products, arithmetic and copies ran while one was open for 30% -> 0% of each run, Pallas kernels for 0% -> 0%
where the time goes in v1:
time: 61.1 us; the launch traced here: 60.8 us
  Pallas kernels  58.8 us (96%)
  other arithmetic  1.39 us (2%)
  between operations  0.64 us (1%)
    pallas_call x1, Pallas kernels, per_device(): pl.pallas_call(functools.partial(exchange_kernel, nr, nf), out_shape=(jax...  42.2 us
    pallas_call x1, Pallas kernels, per_device(): pl.pallas_call(functools.partial(image_kernel, nr * nf), grid=(eb // rows...  16.6 us
    concatenate x1, other arithmetic, per_device(): jnp.concatenate([pair_local, send_block, pair_local, send_block])  1.39 us

profile of v1, /device:TPU:0, one launch (start us, length us, event | category | flops | bytes accessed | tf_op | source)
XLA Modules:
  0.0 60.8 jit_solution(4280474637356774229)
XLA Ops:
  0.6 1.4 %pad_add_fusion = s32[256]{0:T(256)} fusion(s32[64]{0:T(128)} %param.16, s32[64]{0:T(128)} %param.15), kind=kLoop, calls=%fused_computation | loop fusion | flops 768 | bytes 1536 | tf_op jit(solution)/shard_map/concatenate | solution.py:448
  2.0 42.2 %exchange.1 = (f32[1024,128]{1,0:T(8,128)}, bf16[16,256,128]{2,1,0:T(8,128)(2,1)}, f32[24,128]{1,0:T(8,128)}, f32[24,128]{1,0:T(8,128)}) custom-call(f32[3,1024,128]{2,1,0:T(8,128)} %jumps_hbm.1, f32[1024,128]{1,0:T(8,128)} %base_hbm.1, f32[16,1024,128]{2,1,0:T(8,128)} %pr_ref.1, bf16[64,128,128]{2,1,0:T(8,128)(2,1)} %tiles_hbm.1, s32[16,128]{1,0:T(8,128)} %bitcast.8, ...), custom_call_target="tpu_custom_call" | custom-call | tf_op jit(solution)/shard_map/exchange/pallas_call | solution.py:453
  44.2 16.6 %image.1 = (f32[16,1024,128]{2,1,0:T(8,128)}, f32[1024,128]{1,0:T(8,128)}) custom-call(f32[16,1024,128]{2,1,0:T(8,128)} %pr_ref.1, f32[16,1024,128]{2,1,0:T(8,128)} %pr_ref.1, f32[16,1024,128]{2,1,0:T(8,128)} %pr_ref.1, f32[1024,128]{1,0:T(8,128)} %get-tuple-element.6.a_ref.al_ref.ar_ref, f32[1024,128]{1,0:T(8,128)} %get-tuple-element.6.a_ref.al_ref.ar_ref, ...), custom_call_target="tpu_custom_call" | custom-call | tf_op jit(solution)/shard_map/image/pallas_call | solution.py:516

commit v2 on v1

--- a/solution.py
+++ b/solution.py
@@ -137,7 +137,7 @@
         gap[rows, :] = split_lanes(0.5 * soft + 0.2 * (jnp.sqrt(1.0 + b * b + c * c) - 1.0))
         return 0
 
-    lax.fori_loop(0, eb // LANES, gap_step, 0)
+    lax.fori_loop(0, eb // LANES, gap_step, 0, unroll=2)
 
     def face_rows(peer, m):
         row = face_ref[pl.ds(peer * nsub + m, 1), :]
@@ -158,14 +158,15 @@
 
     pl.semaphore_wait(barrier, nr - 1 + nf - 1 + 2)
 
-    def face_step(k, _):
-        peer = lax.rem(me_r + 1 + k // nsub, nr)
-        m = lax.rem(k, nsub)
-        face_out[peer, sub(m), :] = face_rows(peer, m)
-        face_copy(peer, m, me_r).start()
+    def face_step(d, _):
+        peer = lax.rem(me_r + d, nr)
+        for m in range(nsub):
+            face_out[peer, m * LANES : (m + 1) * LANES, :] = face_rows(peer, m)
+        for m in range(nsub):
+            face_copy(peer, m, me_r).start()
         return 0
 
-    lax.fori_loop(0, (nr - 1) * nsub, face_step, 0)
+    lax.fori_loop(1, nr, face_step, 0)
 
     for g in range(2 * slots // LANES):
         pair_hot[g * LANES : (g + 1) * LANES, :] = one_hot(
@@ -179,7 +180,7 @@
         far_out[:, v] = picked[slots:].reshape(nf, cap, width)
         return 0
 
-    lax.fori_loop(0, nv, press_step, 0)
+    lax.fori_loop(0, nv, press_step, 0, unroll=4)
 
     def far_copy(peer, slot):
         return pltpu.make_async_remote_copy(
@@ -195,11 +196,8 @@
         far_copy(lax.rem(me_f + d, nf), me_f).start()
     far_in[me_f] = far_out[me_f]
 
-    def own_step(m, _):
-        face_in[me_r, sub(m), :] = face_rows(me_r, m)
-        return 0
-
-    lax.fori_loop(0, nsub, own_step, 0)
+    for m in range(nsub):
+        face_in[me_r, m * LANES : (m + 1) * LANES, :] = face_rows(me_r, m)
 
     def elem_step(k, _):
         col = column(elem_ref[pl.ds(k, 1), :])
@@ -207,7 +205,7 @@
             elem_hot[s, sub(k), :] = one_hot(col - s * capf, capf)
         return 0
 
-    lax.fori_loop(0, eb // LANES, elem_step, 0)
+    lax.fori_loop(0, eb // LANES, elem_step, 0, unroll=2)
 
     loads[1].wait()
     acc[...] = base[...]
@@ -219,7 +217,7 @@
             acc[sub(k), :] += fold(dot(elem_hot[s, sub(k), :], faces))
             return 0
 
-        lax.fori_loop(0, eb // LANES, step, 0)
+        lax.fori_loop(0, eb // LANES, step, 0, unroll=4)
 
     take(me_r)
     for d in range(1, nr):
@@ -323,8 +321,9 @@
 
     for v in range(nv):
         hi, lo = split(near_term[:, v].reshape(slots, width))
-        terms_ref[v, :slots, :] = hi
-        terms_ref[v, 2 * slots : 3 * slots, :] = lo
+        pair, lanes = v // 2, slice(v % 2 * width, (v % 2 + 1) * width)
+        terms_ref[pair, :slots, lanes] = hi
+        terms_ref[pair, 2 * slots : 3 * slots, lanes] = lo
 
     for d in range(1, nf):
         q = lax.rem(me_f + nf - d, nf)
@@ -332,8 +331,9 @@
 
     for v in range(nv):
         hi, lo = split(ret_in[:, v].reshape(slots, width))
-        terms_ref[v, slots : 2 * slots, :] = hi
-        terms_ref[v, 3 * slots :, :] = lo
+        pair, lanes = v // 2, slice(v % 2 * width, (v % 2 + 1) * width)
+        terms_ref[pair, slots : 2 * slots, lanes] = hi
+        terms_ref[pair, 3 * slots :, lanes] = lo
 
     for edge in edges:
         edge.wait()
@@ -414,16 +414,27 @@
     joined_prv = jnp.where(fr_prv == fr[:1, :], 1.0, 0.0) * has_left
     h_prv = harmonic(t_prv, pltpu.roll(t[:8], width - 1, 1)[:1]) * joined_prv
 
+    h_dn = down(h, h_prv)
+    centre = a + h + h_dn
+    one = jnp.minimum(i, 0) + 1
+    edge = lax.broadcasted_iota(jnp.int32, (8, width), 0)
+
     ids = i * rows + lax.broadcasted_iota(jnp.int32, (rows, slot_ref.shape[1]), 0)
     hot = jnp.where(ids == slot_ref[...], 1.0, 0.0).astype(BF16)
 
     for v in range(nv):
+        if v % 2 == 0:
+            cross = dot(hot, terms_ref[v // 2])
         p = p_ref[v]
         p_prv = jnp.where(first, left_ref[v : v + 1, :], pl_ref[v, halo - 1 :, :])
         p_nxt = jnp.where(last, right_ref[v : v + 1, :], pr_ref[v, :1, :])
-        flux = h * (p - up(p, p_nxt))
-        flux_prv = h_prv * (p_prv - pltpu.roll(p[:8], width - 1, 1)[:1])
-        out_ref[v] = a * p + flux - down(flux, flux_prv) + dot(hot, terms_ref[v])
+        tail = jnp.where(edge == 7, p_nxt, pltpu.roll(p[rows - 8 :], 7, 0))
+        head = jnp.where(edge == 0, p_prv, pltpu.roll(p[:8], 1, 0))
+        below = jnp.concatenate([p_ref[v, pl.ds(one, rows - 8), :], tail], axis=0)
+        above = jnp.concatenate([head, p_ref[v, pl.ds(one + 6, rows - 8), :]], axis=0)
+        p_up = pltpu.roll(jnp.where(first_lane, below, p), width - 1, 1)
+        p_dn = pltpu.roll(jnp.where(last_lane, above, p), 1, 1)
+        out_ref[v] = centre * p - h * p_up - h_dn * p_dn + cross[:, v % 2 * width :][:, :width]
 
 
 def per_device(
@@ -454,7 +465,7 @@
         functools.partial(exchange_kernel, nr, nf),
         out_shape=(
             jax.ShapeDtypeStruct((eb, width), F32),
-            jax.ShapeDtypeStruct((nv, 4 * slots, width), BF16),
+            jax.ShapeDtypeStruct((nv // 2, 4 * slots, 2 * width), BF16),
             jax.ShapeDtypeStruct((edge_rows, width), F32),
             jax.ShapeDtypeStruct((edge_rows, width), F32),
         ),

time: 61.1 us -> 54 us (0.88)
  Pallas kernels: 58.8 us -> 51.6 us
    pallas_call x1, Pallas kernels: 16.6 us -> 11.7 us  [per_device(): pl.pallas_call(functools.partial(image_kernel, nr * nf), grid=(eb // rows...]
    pallas_call x1, Pallas kernels: 42.2 us -> 40 us  [per_device(): pl.pallas_call(functools.partial(exchange_kernel, nr, nf), out_shape=(jax...]
where the time goes in v2:
time: 54 us; the launch traced here: 53.6 us
  Pallas kernels  51.6 us (96%)
  other arithmetic  1.39 us (3%)
  between operations  0.64 us (1%)
    pallas_call x1, Pallas kernels, per_device(): pl.pallas_call(functools.partial(exchange_kernel, nr, nf), out_shape=(jax...  40 us
    pallas_call x1, Pallas kernels, per_device(): pl.pallas_call(functools.partial(image_kernel, nr * nf), grid=(eb // rows...  11.7 us
    concatenate x1, other arithmetic, per_device(): jnp.concatenate([pair_local, send_block, pair_local, send_block])  1.39 us

profile of v2, /device:TPU:0, one launch (start us, length us, event | category | flops | bytes accessed | tf_op | source)
XLA Modules:
  0.0 53.6 jit_solution(2464407272939917589)
XLA Ops:
  0.6 1.4 %pad_add_fusion = s32[256]{0:T(256)} fusion(s32[64]{0:T(128)} %param.16, s32[64]{0:T(128)} %param.15), kind=kLoop, calls=%fused_computation | loop fusion | flops 768 | bytes 1536 | tf_op jit(solution)/shard_map/concatenate | solution.py:459
  2.0 40.0 %exchange.1 = (f32[1024,128]{1,0:T(8,128)}, bf16[8,256,256]{2,1,0:T(8,128)(2,1)}, f32[24,128]{1,0:T(8,128)}, f32[24,128]{1,0:T(8,128)}) custom-call(f32[3,1024,128]{2,1,0:T(8,128)} %jumps_hbm.1, f32[1024,128]{1,0:T(8,128)} %base_hbm.1, f32[16,1024,128]{2,1,0:T(8,128)} %pr_ref.1, bf16[64,128,128]{2,1,0:T(8,128)(2,1)} %tiles_hbm.1, s32[16,128]{1,0:T(8,128)} %bitcast.8, ...), custom_call_target="tpu_custom_call" | custom-call | tf_op jit(solution)/shard_map/exchange/pallas_call | solution.py:464
  42.0 11.7 %image.1 = (f32[16,1024,128]{2,1,0:T(8,128)}, f32[1024,128]{1,0:T(8,128)}) custom-call(f32[16,1024,128]{2,1,0:T(8,128)} %pr_ref.1, f32[16,1024,128]{2,1,0:T(8,128)} %pr_ref.1, f32[16,1024,128]{2,1,0:T(8,128)} %pr_ref.1, f32[1024,128]{1,0:T(8,128)} %get-tuple-element.6.a_ref.al_ref.ar_ref, f32[1024,128]{1,0:T(8,128)} %get-tuple-element.6.a_ref.al_ref.ar_ref, ...), custom_call_target="tpu_custom_call" | custom-call | tf_op jit(solution)/shard_map/image/pallas_call | solution.py:527
